TPU v7x, 128 devices: a whole 4x4x4 slice. The times are simulated.
128 devices in a mesh: slab: 8 (over z, x_lo), view: 16 (over y, x_hi, core).
Axes of the slice: x: 4 (x_hi: 2, x_lo: 2; x = x_hi * 2 + x_lo), y: 4, z: 4, core: 2. Of those that a mesh axis runs over, the one named last changes fastest.
Arguments:
- volume: float32 [128, 32768], P(None, 'slab'), may hold values from 0 to 1
- measured: bfloat16 [32, 128, 2048], P('view'), may hold values from 0 to 8
- weights: bfloat16 [32, 32768, 1024], P('view', 'slab'), as said below
- offsets: int32 [32, 8], P('view', 'slab'), may hold values from 0 to 1024
- order: int32 [32], P('view'), may hold values from 0 to 1, as said below
Outputs:
- updated: float32 [128, 32768], P(None, 'slab')
- mismatch: float32 [32, 128, 2048], P('view')
Inputs may be any that keep to these rules, and one draw needn't show every extreme that they name: `order`: each aligned group of 2 entries is a permutation of 0 to 1. `weights`: every weight is zero or positive, and every voxel has a positive weight in every view.
All inputs are finite; a program needn't handle non-finite values.
Results may differ from a plain program's by a relative error of at most 0.00055.
Values sent between devices are 32-bit elements; how exact they have to be, the bound alone decides.
A program may use at most 128 MiB of HBM per device.

v0:
```python
import jax
import jax.numpy as jnp
from jax import lax
from jax.sharding import PartitionSpec as P

RELAXATION = 0.9


def in_blocks(array, dim, length):
    before, after = (array.shape[:dim], array.shape[dim + 1 :])
    return jnp.moveaxis(array.reshape(*before, length, -1, *after), dim, 0)


def sent_and_summed(array, axis, dim):
    tiles = in_blocks(array, dim, lax.axis_size(axis))
    arrived = lax.all_to_all(tiles, axis, split_axis=0, concat_axis=0, tiled=True)
    return arrived.sum(axis=0)


def sent_to_all(array, axis):
    length = lax.axis_size(axis)
    return lax.all_to_all(
        jnp.broadcast_to(array[None], (length, *array.shape)), axis, 0, 0, tiled=True
    )


def joined_along(tiles, dim):
    tiles = jnp.moveaxis(tiles, 0, dim)
    lengths = tiles.shape
    return tiles.reshape(*lengths[:dim], lengths[dim] * lengths[dim + 1], *lengths[dim + 2 :])


def collect(array, axis, dim):
    tiles = sent_to_all(array, axis)
    return joined_along(tiles, dim)


def per_device(volume, measured, weights, offsets, order):
    subsets = weights.shape[0]
    band_width = weights.shape[2]
    slice_rows = measured.shape[1]
    detector_cols = measured.shape[2]
    mismatch = jnp.zeros(measured.shape, jnp.float32)
    for subset_index in range(subsets):
        chosen_view = order[subset_index]
        footprint = lax.dynamic_index_in_dim(weights, chosen_view, 0, keepdims=False)
        first_column = offsets[chosen_view, 0]
        observed = lax.dynamic_index_in_dim(measured, chosen_view, 0, keepdims=False).astype(
            jnp.float32
        )
        partial_value = jnp.dot(
            volume.astype(jnp.bfloat16), footprint, preferred_element_type=jnp.float32
        )
        placed = lax.dynamic_update_slice(
            jnp.zeros((slice_rows, detector_cols), jnp.float32),
            partial_value,
            (jnp.int32(0), first_column),
        )
        placed_row = lax.dynamic_update_slice(
            jnp.zeros((detector_cols,), jnp.float32),
            jnp.sum(footprint, axis=0, dtype=jnp.float32),
            (first_column,),
        )
        projection_part, row_part = (
            sent_and_summed(placed, "slab", 1),
            sent_and_summed(placed_row, "slab", 0),
        )
        share_width = projection_part.shape[1]
        observed_part = lax.dynamic_slice_in_dim(
            observed, lax.axis_index("slab") * share_width, share_width, 1
        )
        correction_part = (observed_part - projection_part) / jnp.maximum(row_part, 1.0)
        correction = collect(correction_part, "slab", 1)
        mismatch = lax.dynamic_update_index_in_dim(mismatch, correction, chosen_view, 0)
        band_values = lax.dynamic_slice_in_dim(correction, first_column, band_width, 1).astype(
            jnp.bfloat16
        )
        back_terms = lax.dot_general(
            band_values, footprint, (((1,), (1,)), ((), ())), preferred_element_type=jnp.float32
        )
        col_total = jnp.sum(footprint, axis=1, dtype=jnp.float32)
        back_part, weight_part = (
            sent_and_summed(back_terms, "view", 1),
            sent_and_summed(col_total, "view", 0),
        )
        share_width = back_part.shape[1]
        volume_part = lax.dynamic_slice_in_dim(
            volume, lax.axis_index("view") * share_width, share_width, 1
        )
        new_part = volume_part + RELAXATION * back_part / weight_part[None, :]
        volume = lax.all_gather(new_part, "view", axis=1, tiled=True)
    return (volume, mismatch)


def solution(mesh):
    placed = (
        P(None, "slab"),
        P("view", None, None),
        P("view", "slab", None),
        P("view", "slab"),
        P("view"),
    )
    return jax.shard_map(
        per_device,
        mesh=mesh,
        in_specs=placed,
        out_specs=(P(None, "slab"), P("view", None, None)),
        check_vma=False,
    )
```

profile of v0, /device:TPU:1, one launch (start us, length us, event | category | flops | bytes accessed | tf_op | source)
XLA Modules:
  0.0 338.8 jit_solution(11723134778477959800)
XLA Ops:
  7.2 1.3 fusion.17
  12.4 1.4 constant_dynamic-slice_fusion
  15.0 13.8 %convert_reduce_fusion.2 = (f32[4096]{0:T(1024)}, f32[1024]{0:T(1024)S(1)}, bf16[1,4096,1024]{2,1,0:T(8,128)(2,1)}, f32[1024]{0:T(1024)S(1)}, f32[4096]{0:T(1024)}, /*index=5*/bf16[1,4096,1024]{2,1,0:T(8,128)(2,1)}) fusion(bf16[2,4096,1024]{2,1,0:T(8,128)(2,1)} %param.7, s32[]{:T(128)S(6)} %select_n.34, s32[]{:T(128)S(6)} %select_n.37), kind=kLoop, calls=%fused_computation.2 | loop fusion | flops 25155584 | bytes 33595400 | tf_op jit(solution)/shard_map/reduce_sum | solution.py:81
  30.0 1.4 dynamic_update_slice.20
  31.5 6.8 %all-to-all-start.1 = ((f32[8,1,256]{2,1,0:T(1,128)}), f32[8,1,256]{2,1,0:T(1,128)S(1)}, u32[]{:S(2)}, u32[]{:S(2)}) async-start(f32[8,1,256]{2,1,0:T(1,128)} %bitcast.7), calls=%async_computation.1 | async-start | bytes 16384 | tf_op jit(solution)/shard_map/all_to_all | solution.py:16
  38.3 5.7 %fusion.4 = f32[128,1024]{0,1:T(8,128)S(1)} fusion(bf16[1,4096,1024]{2,1,0:T(8,128)(2,1)} %get-tuple-element.7, f32[128,4096]{1,0:T(8,128)S(1)} %copy-done), kind=kOutput, calls=%fused_computation.10 | convolution fusion | flops 1074266112 | bytes 11010048 | tf_op jit(solution)/shard_map/dot_general | solution.py:51
  45.1 3.0 dynamic_update_slice.19
  48.0 5.1 %all-to-all-start = ((f32[8,128,256]{1,2,0:T(8,128)}), f32[8,128,256]{1,2,0:T(8,128)S(1)}, u32[]{:S(2)}, u32[]{:S(2)}) async-start(f32[8,128,256]{1,2,0:T(8,128)} %bitcast.6), calls=%async_computation | async-start | bytes 2097152 | tf_op jit(solution)/shard_map/all_to_all | solution.py:16
  54.1 13.0 %all-to-all-done = f32[8,128,256]{1,2,0:T(8,128)S(1)} async-done(((f32[8,128,256]{1,2,0:T(8,128)}), f32[8,128,256]{1,2,0:T(8,128)S(1)}, u32[]{:S(2)}, u32[]{:S(2)}) %all-to-all-start) | async-done | bytes 1048608 | tf_op jit(solution)/shard_map/all_to_all | solution.py:16
  67.5 18.1 %all_to_all.66 = f32[8,128,256]{2,1,0:T(8,128)S(1)} all-to-all(f32[8,128,256]{2,1,0:T(8,128)S(1)} %broadcast_in_dim.13), channel_id=1, replica_groups=mesh['slab'=8,'view'=16] {'slab'}, dimensions={0} | all-to-all | bytes 2097152 | tf_op jit(solution)/shard_map/all_to_all | solution.py:22
  85.6 9.1 %all-to-all-start.4 = ((f32[16,1,256]{2,1,0:T(1,128)}), f32[16,1,256]{2,1,0:T(1,128)S(1)}, u32[]{:S(2)}, u32[]{:S(2)}) async-start(f32[16,1,256]{2,1,0:T(1,128)} %bitcast.13), calls=%async_computation.4 | async-start | bytes 32768 | tf_op jit(solution)/shard_map/all_to_all | solution.py:16
  94.7 7.6 %convolution_bitcast_fusion.1 = f32[16,128,256]{2,1,0:T(8,128)} fusion(bf16[16,256,1024]{2,1,0:T(8,128)(2,1)} %bitcast.63, bf16[128,2048]{1,0:T(8,128)(2,1)S(1)} %bitcast.68, s32[]{:T(128)S(6)} %select_n.36), kind=kOutput, calls=%fused_computation.9 | convolution fusion | flops 1073741824 | bytes 10747908 | tf_op jit(solution)/shard_map/dot_general | solution.py:78
  102.3 7.2 %all-to-all-start.3 = ((f32[16,128,256]{2,1,0:T(8,128)}), f32[16,128,256]{2,1,0:T(8,128)S(1)}, u32[]{:S(2)}, u32[]{:S(2)}) async-start(f32[16,128,256]{2,1,0:T(8,128)} %convolution_bitcast_fusion.1), calls=%async_computation.3 | async-start | bytes 4194304 | tf_op jit(solution)/shard_map/all_to_all | solution.py:16
  109.6 28.4 %all-to-all-done.3 = f32[16,128,256]{2,1,0:T(8,128)S(1)} async-done(((f32[16,128,256]{2,1,0:T(8,128)}), f32[16,128,256]{2,1,0:T(8,128)S(1)}, u32[]{:S(2)}, u32[]{:S(2)}) %all-to-all-start.3) | async-done | bytes 2097184 | tf_op jit(solution)/shard_map/all_to_all | solution.py:16
  138.1 1.6 divide_add_fusion.1
  142.2 1.4 dynamic_update_slice.22
  143.6 3.3 all-to-all-start.6
  147.0 36.2 %all-gather.3.cloned.1.call-done = f32[128,4096]{1,0:T(8,128)} async-done(((f32[128,256]{1,0:T(8,128)}), f32[128,4096]{1,0:T(8,128)}) %all-gather.3.cloned.1.call-update) | async-done | bytes 2097168 | tf_op jit(solution)/shard_map/all_gather | solution.py:91
  183.1 7.4 %fusion = f32[128,1024]{0,1:T(8,128)S(1)} fusion(bf16[1,4096,1024]{2,1,0:T(8,128)(2,1)} %get-tuple-element.10, f32[128,4096]{1,0:T(8,128)} %all-gather.3.cloned.1.call-done), kind=kOutput, calls=%fused_computation.4 | convolution fusion | flops 1074266112 | bytes 11010048 | tf_op jit(solution)/shard_map/dot_general | solution.py:51
  191.6 3.0 dynamic_update_slice.21
  194.5 4.2 %all-to-all-start.5 = ((f32[8,128,256]{1,2,0:T(8,128)}), f32[8,128,256]{1,2,0:T(8,128)S(1)}, u32[]{:S(2)}, u32[]{:S(2)}) async-start(f32[8,128,256]{1,2,0:T(8,128)} %bitcast.19), calls=%async_computation.5 | async-start | bytes 2097152 | tf_op jit(solution)/shard_map/all_to_all | solution.py:16
  198.8 15.2 %all-to-all-done.5 = f32[8,128,256]{1,2,0:T(8,128)S(1)} async-done(((f32[8,128,256]{1,2,0:T(8,128)}), f32[8,128,256]{1,2,0:T(8,128)S(1)}, u32[]{:S(2)}, u32[]{:S(2)}) %all-to-all-start.5) | async-done | bytes 1048608 | tf_op jit(solution)/shard_map/all_to_all | solution.py:16
  214.4 18.1 %all_to_all.67 = f32[8,128,256]{2,1,0:T(8,128)S(1)} all-to-all(f32[8,128,256]{2,1,0:T(8,128)S(1)} %broadcast_in_dim.14), channel_id=1, replica_groups=mesh['slab'=8,'view'=16] {'slab'}, dimensions={0} | all-to-all | bytes 2097152 | tf_op jit(solution)/shard_map/all_to_all | solution.py:22
  232.5 6.2 %all-to-all-start.9 = ((f32[16,1,256]{2,1,0:T(1,128)}), f32[16,1,256]{2,1,0:T(1,128)S(1)}, u32[]{:S(2)}, u32[]{:S(2)}) async-start(f32[16,1,256]{2,1,0:T(1,128)} %bitcast.26), calls=%async_computation.9 | async-start | bytes 32768 | tf_op jit(solution)/shard_map/all_to_all | solution.py:16
  238.8 7.6 %convolution_bitcast_fusion = f32[16,128,256]{2,1,0:T(8,128)} fusion(bf16[16,256,1024]{2,1,0:T(8,128)(2,1)} %bitcast.62, bf16[128,2048]{1,0:T(8,128)(2,1)S(1)} %bitcast.69, s32[]{:T(128)S(6)} %select_n.38), kind=kOutput, calls=%fused_computation.8 | convolution fusion | flops 1073741824 | bytes 10747908 | tf_op jit(solution)/shard_map/dot_general | solution.py:78
  246.4 7.2 %all-to-all-start.8 = ((f32[16,128,256]{2,1,0:T(8,128)}), f32[16,128,256]{2,1,0:T(8,128)}, u32[]{:S(2)}, u32[]{:S(2)}) async-start(f32[16,128,256]{2,1,0:T(8,128)} %convolution_bitcast_fusion), calls=%async_computation.8 | async-start | bytes 4194304 | tf_op jit(solution)/shard_map/all_to_all | solution.py:16
  253.7 28.5 %all-to-all-done.8 = f32[16,128,256]{2,1,0:T(8,128)} async-done(((f32[16,128,256]{2,1,0:T(8,128)}), f32[16,128,256]{2,1,0:T(8,128)}, u32[]{:S(2)}, u32[]{:S(2)}) %all-to-all-start.8) | async-done | bytes 2097184 | tf_op jit(solution)/shard_map/all_to_all | solution.py:16
  282.2 1.7 reduce_sum.117
  283.9 1.6 divide_add_fusion
  286.2 1.6 broadcast_in_dim.28
  290.6 38.3 %all-gather.5.cloned.1.call-done = f32[128,4096]{1,0:T(8,128)} async-done(((f32[128,256]{1,0:T(8,128)}), f32[128,4096]{1,0:T(8,128)}) %all-gather.5.cloned.1.call-update) | async-done | bytes 2097168 | tf_op jit(solution)/shard_map/all_gather | solution.py:91
  328.9 3.1 copy.76
  (40 shorter events, 9.0 us)
Async XLA Ops:
  15.0 23.3 %copy-start = (f32[128,4096]{1,0:T(8,128)S(1)}, f32[128,4096]{1,0:T(8,128)}, u32[]{:S(2)}) copy-start(f32[128,4096]{1,0:T(8,128)} %param.5) | copy-start | bytes 6291460
  31.5 16.5 %all-to-all-start.1 = ((f32[8,1,256]{2,1,0:T(1,128)}), f32[8,1,256]{2,1,0:T(1,128)S(1)}, u32[]{:S(2)}, u32[]{:S(2)}) async-start(f32[8,1,256]{2,1,0:T(1,128)} %bitcast.7), calls=%async_computation.1 | async-start | bytes 16384 | tf_op jit(solution)/shard_map/all_to_all | solution.py:16
  48.0 19.1 %all-to-all-start = ((f32[8,128,256]{1,2,0:T(8,128)}), f32[8,128,256]{1,2,0:T(8,128)S(1)}, u32[]{:S(2)}, u32[]{:S(2)}) async-start(f32[8,128,256]{1,2,0:T(8,128)} %bitcast.6), calls=%async_computation | async-start | bytes 2097152 | tf_op jit(solution)/shard_map/all_to_all | solution.py:16
  85.6 16.7 %all-to-all-start.4 = ((f32[16,1,256]{2,1,0:T(1,128)}), f32[16,1,256]{2,1,0:T(1,128)S(1)}, u32[]{:S(2)}, u32[]{:S(2)}) async-start(f32[16,1,256]{2,1,0:T(1,128)} %bitcast.13), calls=%async_computation.4 | async-start | bytes 32768 | tf_op jit(solution)/shard_map/all_to_all | solution.py:16
  102.3 35.7 %all-to-all-start.3 = ((f32[16,128,256]{2,1,0:T(8,128)}), f32[16,128,256]{2,1,0:T(8,128)S(1)}, u32[]{:S(2)}, u32[]{:S(2)}) async-start(f32[16,128,256]{2,1,0:T(8,128)} %convolution_bitcast_fusion.1), calls=%async_computation.3 | async-start | bytes 4194304 | tf_op jit(solution)/shard_map/all_to_all | solution.py:16
  109.5 73.6 %all-gather.3.cloned.1.call-start = ((), (), s32[]{:S(2)}) async-start(), calls=%async_computation.10 | async-start | bytes 2228224 | tf_op jit(solution)/shard_map/all_gather | solution.py:91
  143.6 50.9 %all-to-all-start.6 = ((f32[8,1,256]{2,1,0:T(1,128)}), f32[8,1,256]{2,1,0:T(1,128)S(1)}, u32[]{:S(2)}, u32[]{:S(2)}) async-start(f32[8,1,256]{2,1,0:T(1,128)} %bitcast.20), calls=%async_computation.6 | async-start | bytes 16384 | tf_op jit(solution)/shard_map/all_to_all | solution.py:16
  194.5 19.5 %all-to-all-start.5 = ((f32[8,128,256]{1,2,0:T(8,128)}), f32[8,128,256]{1,2,0:T(8,128)S(1)}, u32[]{:S(2)}, u32[]{:S(2)}) async-start(f32[8,128,256]{1,2,0:T(8,128)} %bitcast.19), calls=%async_computation.5 | async-start | bytes 2097152 | tf_op jit(solution)/shard_map/all_to_all | solution.py:16
  232.5 13.9 %all-to-all-start.9 = ((f32[16,1,256]{2,1,0:T(1,128)}), f32[16,1,256]{2,1,0:T(1,128)S(1)}, u32[]{:S(2)}, u32[]{:S(2)}) async-start(f32[16,1,256]{2,1,0:T(1,128)} %bitcast.26), calls=%async_computation.9 | async-start | bytes 32768 | tf_op jit(solution)/shard_map/all_to_all | solution.py:16
  246.4 35.8 %all-to-all-start.8 = ((f32[16,128,256]{2,1,0:T(8,128)}), f32[16,128,256]{2,1,0:T(8,128)}, u32[]{:S(2)}, u32[]{:S(2)}) async-start(f32[16,128,256]{2,1,0:T(8,128)} %convolution_bitcast_fusion), calls=%async_computation.8 | async-start | bytes 4194304 | tf_op jit(solution)/shard_map/all_to_all | solution.py:16
  253.6 75.3 %all-gather.5.cloned.1.call-start = ((), (), s32[]{:S(2)}) async-start(), calls=%async_computation.11 | async-start | bytes 2228224 | tf_op jit(solution)/shard_map/all_gather | solution.py:91
Sparse Core Ops, SparseCore 0:
  139.9 43.2 all-gather.2
  285.7 43.1 all-gather.4
where the time goes:
time: 340 us; the launch traced here: 339 us
  waiting for transfers between devices  160 us (47%)
  starting transfers between devices  49.1 us (14%)
  blocking collectives  36.2 us (11%)
  matrix products  28.3 us (8%)
  local copies, waits for them, and re-layouts  23.5 us (7%)
  between operations  21.9 us (6%)
  other arithmetic  20.2 us (6%)
    all_to_all x8, waiting for transfers between devices, sent_and_summed(): lax.all_to_all(tiles, axis, split_axis=0, concat_axis=0, tiled=True)  85.1 us
    all_gather x2, waiting for transfers between devices, per_device(): volume = lax.all_gather(new_part, 'view', axis=1, tiled=True)  74.4 us
    all_to_all x8, starting transfers between devices, sent_and_summed(): lax.all_to_all(tiles, axis, split_axis=0, concat_axis=0, tiled=True)  49.1 us
    all_to_all x2, blocking collectives, sent_to_all(): lax.all_to_all(jnp.broadcast_to(array[None], (length, *array.shape)), axi...  36.2 us
    dot_general x2, matrix products, per_device(): lax.dot_general(band_values, footprint, (((1,), (1,)), ((), ())), preferr...  15.2 us
    reduce_sum x1, other arithmetic, per_device(): col_total = jnp.sum(footprint, axis=1, dtype=jnp.float32)  13.8 us
    dot_general x2, matrix products, per_device(): jnp.dot(volume.astype(jnp.bfloat16), footprint, preferred_element_type=jn...  13.1 us
  transfers between devices with their start and end apart: 10, of which 6 were waited for; matrix products, arithmetic and copies ran while one was open for 13% of the time, Pallas kernels for 0%

commit v1 on v0

--- a/solution.py
+++ b/solution.py
@@ -88,7 +88,9 @@
             volume, lax.axis_index("view") * share_width, share_width, 1
         )
         new_part = volume_part + RELAXATION * back_part / weight_part[None, :]
-        volume = lax.all_gather(new_part, "view", axis=1, tiled=True)
+        volume = jnp.concatenate(
+            lax.all_to_all(jnp.stack([new_part] * lax.axis_size("view")), "view", 0, 0), axis=1
+        )
     return (volume, mismatch)
 
 

time: 340 us -> 316 us (0.929)
  waiting for transfers between devices: 160 us -> 131 us
  between operations: 21.9 us -> 8.53 us
  starting transfers between devices: 49.1 us -> 58.5 us
  local copies, waits for them, and re-layouts: 23.5 us -> 31.4 us
    all_gather x2 -> x0, waiting for transfers between devices: 74.4 us -> none  [per_device(): volume = lax.all_gather(new_part, 'view', axis=1, tiled=True)]
    all_to_all x0 -> x2, waiting for transfers between devices: none -> 48.3 us  [per_device(): lax.all_to_all(jnp.stack([new_part] * lax.axis_size('view')), 'view', 0, 0)]
    all_to_all x0 -> x2, starting transfers between devices: none -> 9.52 us  [per_device(): lax.all_to_all(jnp.stack([new_part] * lax.axis_size('view')), 'view', 0, 0)]
    all_to_all x0 -> x2, local copies, waits for them, and re-layouts: none -> 3.82 us  [per_device(): lax.all_to_all(jnp.stack([new_part] * lax.axis_size('view')), 'view', 0, 0)]
  transfers between devices with their start and end apart: 10 -> 10, of which waited for: 6 -> 6; matrix products, arithmetic and copies ran while one was open for 13% -> 15% of each run, Pallas kernels for 0% -> 0%
where the time goes in v1:
time: 316 us; the launch traced here: 314 us
  waiting for transfers between devices  131 us (41%)
  starting transfers between devices  58.5 us (19%)
  blocking collectives  37.1 us (12%)
  local copies, waits for them, and re-layouts  31.4 us (10%)
  matrix products  29.1 us (9%)
  other arithmetic  18.1 us (6%)
  between operations  8.53 us (3%)
    all_to_all x8, waiting for transfers between devices, sent_and_summed(): lax.all_to_all(tiles, axis, split_axis=0, concat_axis=0, tiled=True)  83.1 us
    all_to_all x8, starting transfers between devices, sent_and_summed(): lax.all_to_all(tiles, axis, split_axis=0, concat_axis=0, tiled=True)  49 us
    all_to_all x2, waiting for transfers between devices, per_device(): lax.all_to_all(jnp.stack([new_part] * lax.axis_size('view')), 'view', 0, 0)  48.3 us
    all_to_all x2, blocking collectives, sent_to_all(): lax.all_to_all(jnp.broadcast_to(array[None], (length, *array.shape)), axi...  37.1 us
    dot_general x2, matrix products, per_device(): lax.dot_general(band_values, footprint, (((1,), (1,)), ((), ())), preferr...  15.2 us
    dot_general x2, matrix products, per_device(): jnp.dot(volume.astype(jnp.bfloat16), footprint, preferred_element_type=jn...  13.9 us
    reduce_sum x1, other arithmetic, per_device(): col_total = jnp.sum(footprint, axis=1, dtype=jnp.float32)  13.8 us
    all_to_all x2, starting transfers between devices, per_device(): lax.all_to_all(jnp.stack([new_part] * lax.axis_size('view')), 'view', 0, 0)  9.52 us
  transfers between devices with their start and end apart: 10, of which 6 were waited for; matrix products, arithmetic and copies ran while one was open for 15% of the time, Pallas kernels for 0%

profile of v1, /device:TPU:1, one launch (start us, length us, event | category | flops | bytes accessed | tf_op | source)
XLA Modules:
  0.0 314.1 jit_solution(7474503060446154873)
XLA Ops:
  8.5 13.8 %convert_reduce_fusion = (f32[4096]{0:T(1024)}, f32[1024]{0:T(1024)S(1)}, bf16[1,4096,1024]{2,1,0:T(8,128)(2,1)}, f32[1024]{0:T(1024)S(1)}, f32[4096]{0:T(1024)}, /*index=5*/bf16[1,4096,1024]{2,1,0:T(8,128)(2,1)}) fusion(bf16[2,4096,1024]{2,1,0:T(8,128)(2,1)} %param.7, s32[]{:T(128)S(6)} %select_n.37, s32[]{:T(128)S(6)} %select_n.34), kind=kLoop, calls=%fused_computation | loop fusion | flops 25155584 | bytes 33595400 | tf_op jit(solution)/shard_map/reduce_sum | solution.py:81
  24.9 6.8 %all-to-all-start.1 = ((f32[8,1,256]{2,1,0:T(1,128)}), f32[8,1,256]{2,1,0:T(1,128)S(1)}, u32[]{:S(2)}, u32[]{:S(2)}) async-start(f32[8,1,256]{2,1,0:T(1,128)} %bitcast.7), calls=%async_computation.1 | async-start | bytes 16384 | tf_op jit(solution)/shard_map/all_to_all | solution.py:16
  31.7 5.7 %fusion.4 = f32[128,1024]{0,1:T(8,128)S(1)} fusion(bf16[1,4096,1024]{2,1,0:T(8,128)(2,1)} %get-tuple-element.18, f32[128,4096]{1,0:T(8,128)S(1)} %copy-done.2), kind=kOutput, calls=%fused_computation.11 | convolution fusion | flops 1074266112 | bytes 11010048 | tf_op jit(solution)/shard_map/dot_general | solution.py:51
  38.5 3.0 dynamic_update_slice.19
  41.5 5.1 %all-to-all-start = ((f32[8,128,256]{1,2,0:T(8,128)}), f32[8,128,256]{1,2,0:T(8,128)S(1)}, u32[]{:S(2)}, u32[]{:S(2)}) async-start(f32[8,128,256]{1,2,0:T(8,128)} %bitcast.6), calls=%async_computation | async-start | bytes 2097152 | tf_op jit(solution)/shard_map/all_to_all | solution.py:16
  47.6 13.0 %all-to-all-done = f32[8,128,256]{1,2,0:T(8,128)S(1)} async-done(((f32[8,128,256]{1,2,0:T(8,128)}), f32[8,128,256]{1,2,0:T(8,128)S(1)}, u32[]{:S(2)}, u32[]{:S(2)}) %all-to-all-start) | async-done | bytes 1048608 | tf_op jit(solution)/shard_map/all_to_all | solution.py:16
  60.9 18.1 %all_to_all.76 = f32[8,128,256]{2,1,0:T(8,128)S(1)} all-to-all(f32[8,128,256]{2,1,0:T(8,128)S(1)} %broadcast_in_dim.13), channel_id=1, replica_groups=mesh['slab'=8,'view'=16] {'slab'}, dimensions={0} | all-to-all | bytes 2097152 | tf_op jit(solution)/shard_map/all_to_all | solution.py:22
  79.1 9.1 %all-to-all-start.4 = ((f32[16,1,256]{2,1,0:T(1,128)}), f32[16,1,256]{2,1,0:T(1,128)S(1)}, u32[]{:S(2)}, u32[]{:S(2)}) async-start(f32[16,1,256]{2,1,0:T(1,128)} %bitcast.13), calls=%async_computation.4 | async-start | bytes 32768 | tf_op jit(solution)/shard_map/all_to_all | solution.py:16
  88.2 7.6 %convolution_bitcast_fusion.1 = f32[16,128,256]{2,1,0:T(8,128)} fusion(bf16[16,256,1024]{2,1,0:T(8,128)(2,1)} %bitcast.72, bf16[128,2048]{1,0:T(8,128)(2,1)S(1)} %bitcast.81, s32[]{:T(128)S(6)} %select_n.36), kind=kOutput, calls=%fused_computation.10 | convolution fusion | flops 1073741824 | bytes 10747908 | tf_op jit(solution)/shard_map/dot_general | solution.py:78
  95.8 7.2 %all-to-all-start.3 = ((f32[16,128,256]{2,1,0:T(8,128)}), f32[16,128,256]{2,1,0:T(8,128)S(1)}, u32[]{:S(2)}, u32[]{:S(2)}) async-start(f32[16,128,256]{2,1,0:T(8,128)} %convolution_bitcast_fusion.1), calls=%async_computation.3 | async-start | bytes 4194304 | tf_op jit(solution)/shard_map/all_to_all | solution.py:16
  103.0 28.4 %all-to-all-done.3 = f32[16,128,256]{2,1,0:T(8,128)S(1)} async-done(((f32[16,128,256]{2,1,0:T(8,128)}), f32[16,128,256]{2,1,0:T(8,128)S(1)}, u32[]{:S(2)}, u32[]{:S(2)}) %all-to-all-start.3) | async-done | bytes 2097184 | tf_op jit(solution)/shard_map/all_to_all | solution.py:16
  132.5 1.5 stack.4
  134.1 4.4 %all-to-all-start.5 = ((f32[16,128,256]{2,1,0:T(8,128)}), f32[16,128,256]{2,1,0:T(8,128)S(1)}, u32[]{:S(2)}, u32[]{:S(2)}) async-start(f32[16,128,256]{2,1,0:T(8,128)} %stack.4), calls=%async_computation.5 | async-start | bytes 4194304 | tf_op jit(solution)/shard_map/all_to_all | solution.py:92
  142.3 24.7 %all-to-all-done.5 = f32[16,128,256]{2,1,0:T(8,128)S(1)} async-done(((f32[16,128,256]{2,1,0:T(8,128)}), f32[16,128,256]{2,1,0:T(8,128)S(1)}, u32[]{:S(2)}, u32[]{:S(2)}) %all-to-all-start.5) | async-done | bytes 2097184 | tf_op jit(solution)/shard_map/all_to_all | solution.py:92
  168.4 3.5 %all-to-all-start.7 = ((f32[8,1,256]{2,1,0:T(1,128)}), f32[8,1,256]{2,1,0:T(1,128)S(1)}, u32[]{:S(2)}, u32[]{:S(2)}) async-start(f32[8,1,256]{2,1,0:T(1,128)} %bitcast.23), calls=%async_computation.7 | async-start | bytes 16384 | tf_op jit(solution)/shard_map/all_to_all | solution.py:16
  171.9 1.9 copy.68
  174.0 8.2 %fusion = f32[128,1024]{0,1:T(8,128)} fusion(bf16[128,4096]{0,1:T(8,128)(2,1)S(1)} %bitcast.77, bf16[1,4096,1024]{2,1,0:T(8,128)(2,1)} %get-tuple-element.14), kind=kOutput, calls=%fused_computation.4 | convolution fusion | flops 1073741824 | bytes 9961472 | tf_op jit(solution)/shard_map/dot_general | solution.py:51
  183.2 3.0 dynamic_update_slice.21
  186.2 4.9 %all-to-all-start.6 = ((f32[8,128,256]{1,2,0:T(8,128)}), f32[8,128,256]{1,2,0:T(8,128)S(1)}, u32[]{:S(2)}, u32[]{:S(2)}) async-start(f32[8,128,256]{1,2,0:T(8,128)} %bitcast.78), calls=%async_computation.6 | async-start | bytes 2097152 | tf_op jit(solution)/shard_map/all_to_all | solution.py:16
  191.2 14.1 %all-to-all-done.6 = f32[8,128,256]{1,2,0:T(8,128)S(1)} async-done(((f32[8,128,256]{1,2,0:T(8,128)}), f32[8,128,256]{1,2,0:T(8,128)S(1)}, u32[]{:S(2)}, u32[]{:S(2)}) %all-to-all-start.6) | async-done | bytes 1048608 | tf_op jit(solution)/shard_map/all_to_all | solution.py:16
  205.7 18.9 %all_to_all.77 = f32[8,128,256]{2,1,0:T(8,128)S(1)} all-to-all(f32[8,128,256]{2,1,0:T(8,128)S(1)} %broadcast_in_dim.14), channel_id=1, replica_groups=mesh['slab'=8,'view'=16] {'slab'}, dimensions={0} | all-to-all | bytes 2097152 | tf_op jit(solution)/shard_map/all_to_all | solution.py:22
  224.6 5.2 %all-to-all-start.10 = ((f32[16,1,256]{2,1,0:T(1,128)}), f32[16,1,256]{2,1,0:T(1,128)S(1)}, u32[]{:S(2)}, u32[]{:S(2)}) async-start(f32[16,1,256]{2,1,0:T(1,128)} %bitcast.29), calls=%async_computation.10 | async-start | bytes 32768 | tf_op jit(solution)/shard_map/all_to_all | solution.py:16
  229.9 7.6 %convolution_bitcast_fusion = f32[16,128,256]{2,1,0:T(8,128)} fusion(bf16[16,256,1024]{2,1,0:T(8,128)(2,1)} %bitcast.71, bf16[128,2048]{1,0:T(8,128)(2,1)S(1)} %bitcast.82, s32[]{:T(128)S(6)} %select_n.38), kind=kOutput, calls=%fused_computation.9 | convolution fusion | flops 1073741824 | bytes 10747908 | tf_op jit(solution)/shard_map/dot_general | solution.py:78
  237.5 7.2 %all-to-all-start.9 = ((f32[16,128,256]{2,1,0:T(8,128)}), f32[16,128,256]{2,1,0:T(8,128)}, u32[]{:S(2)}, u32[]{:S(2)}) async-start(f32[16,128,256]{2,1,0:T(8,128)} %convolution_bitcast_fusion), calls=%async_computation.9 | async-start | bytes 4194304 | tf_op jit(solution)/shard_map/all_to_all | solution.py:16
  245.8 27.5 %all-to-all-done.9 = f32[16,128,256]{2,1,0:T(8,128)} async-done(((f32[16,128,256]{2,1,0:T(8,128)}), f32[16,128,256]{2,1,0:T(8,128)}, u32[]{:S(2)}, u32[]{:S(2)}) %all-to-all-start.9) | async-done | bytes 2097184 | tf_op jit(solution)/shard_map/all_to_all | solution.py:16
  273.4 1.7 reduce_sum.117
  275.1 1.5 stack.5
  276.6 5.1 %all-to-all-start.11 = ((f32[16,128,256]{2,1,0:T(8,128)}), f32[16,128,256]{2,1,0:T(8,128)}, u32[]{:S(2)}, u32[]{:S(2)}) async-start(f32[16,128,256]{2,1,0:T(8,128)} %stack.5), calls=%async_computation.11 | async-start | bytes 4194304 | tf_op jit(solution)/shard_map/all_to_all | solution.py:92
  282.4 1.6 broadcast_in_dim.28
  286.8 23.6 %all-to-all-done.11 = f32[16,128,256]{2,1,0:T(8,128)} async-done(((f32[16,128,256]{2,1,0:T(8,128)}), f32[16,128,256]{2,1,0:T(8,128)}, u32[]{:S(2)}, u32[]{:S(2)}) %all-to-all-start.11) | async-done | bytes 2097184 | tf_op jit(solution)/shard_map/all_to_all | solution.py:92
  310.4 1.9 copy.77
  312.3 1.8 copy.80
  (49 shorter events, 17.9 us)
Async XLA Ops:
  8.5 23.2 %copy-start.2 = (f32[128,4096]{1,0:T(8,128)S(1)}, f32[128,4096]{1,0:T(8,128)}, u32[]{:S(2)}) copy-start(f32[128,4096]{1,0:T(8,128)} %param.5) | copy-start | bytes 6291460
  24.9 16.5 %all-to-all-start.1 = ((f32[8,1,256]{2,1,0:T(1,128)}), f32[8,1,256]{2,1,0:T(1,128)S(1)}, u32[]{:S(2)}, u32[]{:S(2)}) async-start(f32[8,1,256]{2,1,0:T(1,128)} %bitcast.7), calls=%async_computation.1 | async-start | bytes 16384 | tf_op jit(solution)/shard_map/all_to_all | solution.py:16
  41.5 19.1 %all-to-all-start = ((f32[8,128,256]{1,2,0:T(8,128)}), f32[8,128,256]{1,2,0:T(8,128)S(1)}, u32[]{:S(2)}, u32[]{:S(2)}) async-start(f32[8,128,256]{1,2,0:T(8,128)} %bitcast.6), calls=%async_computation | async-start | bytes 2097152 | tf_op jit(solution)/shard_map/all_to_all | solution.py:16
  79.1 16.7 %all-to-all-start.4 = ((f32[16,1,256]{2,1,0:T(1,128)}), f32[16,1,256]{2,1,0:T(1,128)S(1)}, u32[]{:S(2)}, u32[]{:S(2)}) async-start(f32[16,1,256]{2,1,0:T(1,128)} %bitcast.13), calls=%async_computation.4 | async-start | bytes 32768 | tf_op jit(solution)/shard_map/all_to_all | solution.py:16
  95.8 35.7 %all-to-all-start.3 = ((f32[16,128,256]{2,1,0:T(8,128)}), f32[16,128,256]{2,1,0:T(8,128)S(1)}, u32[]{:S(2)}, u32[]{:S(2)}) async-start(f32[16,128,256]{2,1,0:T(8,128)} %convolution_bitcast_fusion.1), calls=%async_computation.3 | async-start | bytes 4194304 | tf_op jit(solution)/shard_map/all_to_all | solution.py:16
  134.1 33.0 %all-to-all-start.5 = ((f32[16,128,256]{2,1,0:T(8,128)}), f32[16,128,256]{2,1,0:T(8,128)S(1)}, u32[]{:S(2)}, u32[]{:S(2)}) async-start(f32[16,128,256]{2,1,0:T(8,128)} %stack.4), calls=%async_computation.5 | async-start | bytes 4194304 | tf_op jit(solution)/shard_map/all_to_all | solution.py:92
  167.1 1.3 copy-start.1
  168.4 17.8 %all-to-all-start.7 = ((f32[8,1,256]{2,1,0:T(1,128)}), f32[8,1,256]{2,1,0:T(1,128)S(1)}, u32[]{:S(2)}, u32[]{:S(2)}) async-start(f32[8,1,256]{2,1,0:T(1,128)} %bitcast.23), calls=%async_computation.7 | async-start | bytes 16384 | tf_op jit(solution)/shard_map/all_to_all | solution.py:16
  173.8 8.4 %copy-start = (f32[16,128,256]{1,2,0:T(8,128)}, f32[16,128,256]{1,2,0:T(8,128)S(1)}, u32[]{:S(2)}) copy-start(f32[16,128,256]{1,2,0:T(8,128)S(1)} %copy.68) | copy-start | bytes 6291460
  186.2 19.1 %all-to-all-start.6 = ((f32[8,128,256]{1,2,0:T(8,128)}), f32[8,128,256]{1,2,0:T(8,128)S(1)}, u32[]{:S(2)}, u32[]{:S(2)}) async-start(f32[8,128,256]{1,2,0:T(8,128)} %bitcast.78), calls=%async_computation.6 | async-start | bytes 2097152 | tf_op jit(solution)/shard_map/all_to_all | solution.py:16
  224.6 12.9 %all-to-all-start.10 = ((f32[16,1,256]{2,1,0:T(1,128)}), f32[16,1,256]{2,1,0:T(1,128)S(1)}, u32[]{:S(2)}, u32[]{:S(2)}) async-start(f32[16,1,256]{2,1,0:T(1,128)} %bitcast.29), calls=%async_computation.10 | async-start | bytes 32768 | tf_op jit(solution)/shard_map/all_to_all | solution.py:16
  237.5 35.8 %all-to-all-start.9 = ((f32[16,128,256]{2,1,0:T(8,128)}), f32[16,128,256]{2,1,0:T(8,128)}, u32[]{:S(2)}, u32[]{:S(2)}) async-start(f32[16,128,256]{2,1,0:T(8,128)} %convolution_bitcast_fusion), calls=%async_computation.9 | async-start | bytes 4194304 | tf_op jit(solution)/shard_map/all_to_all | solution.py:16
  276.6 33.7 %all-to-all-start.11 = ((f32[16,128,256]{2,1,0:T(8,128)}), f32[16,128,256]{2,1,0:T(8,128)}, u32[]{:S(2)}, u32[]{:S(2)}) async-start(f32[16,128,256]{2,1,0:T(8,128)} %stack.5), calls=%async_computation.11 | async-start | bytes 4194304 | tf_op jit(solution)/shard_map/all_to_all | solution.py:92
